TPU v7x, 32 devices: a whole 2x2x4 slice. The times are simulated.
32 devices in a mesh: groups: 2 (over x), rows: 8 (over z, y), bands: 2 (over core).
Axes of the slice: x: 2, y: 2, z: 4, core: 2. Of those that a mesh axis runs over, the one named last changes fastest.
Arguments:
- radiance: bfloat16 [224, 512, 1024], P('bands', ('groups', 'rows')), parts along dimension 1, may hold values from -6 to 6
- response: bfloat16 [224], P('bands'), may hold values from 0.019897461 to 0.19921875
- reference_tiles: float32 [32, 128, 128], P(('groups', 'rows')), parts along dimension 0, may hold values from -6 to 6
- chip_owner: int32 [60, 1], P('groups'), parts along dimension 0, may hold values from 0 to 7; in each aligned block of 15 rows (0 to 14, 15 to 29, ...) at most 2 rows name the same one
- tile_slot: int32 [60], P('groups'), parts along dimension 0, may hold values from 0 to 1
- row_offset: int32 [60], P('groups'), parts along dimension 0, may hold values from -127 to 127
- column_offset: int32 [60], P('groups'), parts along dimension 0, may hold values from -512 to 511
- valid_rows: int32 [2], P('groups'), parts along dimension 0, may hold values from 128 to 256
Outputs:
- aligned: bfloat16 [224, 512, 1024], P('bands', ('groups', 'rows')), parts along dimension 1
- surface: float32 [512, 1920], P(('groups', 'rows')), parts along dimension 0
There are 2 independent parts, one for each index of `groups`. A program takes and returns all parts, laid end to end along the dimension named above; an argument that names none is the same for every part. Nothing has to cross between parts.
Inputs may be any that keep to these rules, and one draw needn't show every extreme that they name: `chip_owner`: among the 15 chips of one chip row (chips k * 15 to k * 15 + 14) no owner is named more than 2 times, and in some chip row one owner is named exactly 2 times; every owner is named by some chip.
All inputs are finite; a program needn't handle non-finite values.
Results may differ from a plain program's by a relative error of at most 0.011.
Values may be sent and summed in bfloat16 or wider, within the bound.
A program may use at most 128 MiB of HBM per device.

v0:
```python
import math

import jax
import jax.numpy as jnp
from jax import lax
from jax.sharding import PartitionSpec as P

CHIP = 128
MAXDY = 2


highest = lax.Precision.HIGHEST


def for_sending(value):
    return jax.tree.map(lambda a: a.astype(jnp.bfloat16) if a.dtype == jnp.float32 else a, value)


def extended_2(block, sides, width):
    for axis, dim in sides:
        count = lax.axis_size(axis)
        forward = [(i, i + 1) for i in range(count - 1)]
        backward = [(target, source) for source, target in forward]
        low = lax.ppermute(
            lax.slice_in_dim(block, block.shape[dim] - width, None, axis=dim), axis, forward
        )
        high = lax.ppermute(lax.slice_in_dim(block, 0, width, axis=dim), axis, backward)
        block = jnp.concatenate([low, block, high], axis=dim)
    return block


def hann_at(positions, length):
    return 0.5 - 0.5 * jnp.cos(positions * (2.0 * math.pi / length))


def chip_tables(length):
    indices = jnp.arange(length, dtype=jnp.int32)
    angles = (jnp.outer(indices, indices) % length).astype(jnp.float32) * (2.0 * math.pi / length)
    return (jnp.cos(angles), jnp.sin(angles))


def forward_spectra(blocks, cosine_table, sine_table):
    column_real = jnp.einsum("npq,qv->npv", blocks, cosine_table, precision=highest)
    column_imag = -jnp.einsum("npq,qv->npv", blocks, sine_table, precision=highest)
    spec_real = jnp.einsum(
        "up,npv->nuv", cosine_table, column_real, precision=highest
    ) + jnp.einsum("up,npv->nuv", sine_table, column_imag, precision=highest)
    spec_imag = jnp.einsum(
        "up,npv->nuv", cosine_table, column_imag, precision=highest
    ) - jnp.einsum("up,npv->nuv", sine_table, column_real, precision=highest)
    return (spec_real, spec_imag)


def rows_forward(column_real, column_imag, cosine_table, sine_table):
    spec_real = jnp.einsum(
        "up,kmpv->kmuv", cosine_table, column_real, precision=highest
    ) + jnp.einsum("up,kmpv->kmuv", sine_table, column_imag, precision=highest)
    spec_imag = jnp.einsum(
        "up,kmpv->kmuv", cosine_table, column_imag, precision=highest
    ) - jnp.einsum("up,kmpv->kmuv", sine_table, column_real, precision=highest)
    return (spec_real, spec_imag)


def rows_inverse(cross_real, cross_imag, cosine_table, sine_table):
    back_real = jnp.einsum(
        "up,kmpv->kmuv", cosine_table, cross_real, precision=highest
    ) - jnp.einsum("up,kmpv->kmuv", sine_table, cross_imag, precision=highest)
    back_imag = jnp.einsum(
        "up,kmpv->kmuv", cosine_table, cross_imag, precision=highest
    ) + jnp.einsum("up,kmpv->kmuv", sine_table, cross_real, precision=highest)
    return (back_real, back_imag)


def correlate_on_owner(
    column_real, column_imag, chip_picks, tile_real, tile_imag, cosine_table, sine_table
):
    spec_real, spec_imag = rows_forward(column_real, column_imag, cosine_table, sine_table)
    ref_real = jnp.einsum("kmt,tuv->kmuv", chip_picks, tile_real, precision=highest)
    ref_imag = jnp.einsum("kmt,tuv->kmuv", chip_picks, tile_imag, precision=highest)
    cross_real = spec_real * ref_real + spec_imag * ref_imag
    cross_imag = spec_imag * ref_real - spec_real * ref_imag
    return rows_inverse(cross_real, cross_imag, cosine_table, sine_table)


def assemble(cell_rows, per_chip):
    owners, item_count, height, last_size = cell_rows.shape
    grouped = cell_rows.reshape(
        owners // per_chip, per_chip, item_count, height, last_size
    ).transpose(0, 2, 1, 3, 4)
    return grouped.reshape(owners // per_chip, item_count, per_chip * height, last_size)


def first_of_chip(tile_picks, per_chip):
    owners, item_count, tile_count = tile_picks.shape
    return tile_picks.reshape(owners // per_chip, per_chip, item_count, tile_count)[:, 0]


def split_rows(blocks, per_chip):
    groups, item_count, length, last_size = blocks.shape
    height = length // per_chip
    grouped = blocks.reshape(groups, item_count, per_chip, height, last_size).transpose(
        0, 2, 1, 3, 4
    )
    return grouped.reshape(groups * per_chip, item_count, height, last_size)


def keys_kernel(distance):
    magnitude = jnp.abs(distance)
    inner_part = (1.5 * magnitude - 2.5) * magnitude * magnitude + 1.0
    outer_part = ((-0.5 * magnitude + 2.5) * magnitude - 4.0) * magnitude + 2.0
    return jnp.where(magnitude <= 1.0, inner_part, jnp.where(magnitude < 2.0, outer_part, 0.0))


def offset_fields(row_offset, column_offset, across, first_row, row_count):
    chip_rows = row_offset.shape[0] // across
    stacked = jnp.stack([row_offset, column_offset], axis=1).astype(jnp.float32)
    row_means = jnp.sum(stacked.reshape(chip_rows, across, 2), axis=1) / (64.0 * across)
    centres = jnp.arange(chip_rows, dtype=jnp.float32) * CHIP + (CHIP - 1) * 0.5
    positions = first_row + jnp.arange(row_count, dtype=jnp.float32)
    clipped = jnp.clip(positions, centres[0], centres[chip_rows - 1])
    weights = jnp.maximum(1.0 - jnp.abs(clipped[:, None] - centres[None, :]) / CHIP, 0.0)
    return jnp.dot(weights, row_means, precision=highest)


def shift_tables(row_width):
    half_width = row_width // 2
    samples = jnp.arange(row_width, dtype=jnp.int32)
    frequency = jnp.arange(half_width, dtype=jnp.int32)
    angles = (jnp.outer(samples, frequency) % row_width).astype(jnp.float32) * (
        2.0 * math.pi / row_width
    )
    forward = jnp.concatenate([jnp.cos(angles), jnp.sin(angles)], axis=1).astype(jnp.bfloat16)
    scaling = jnp.where(frequency == 0, 1.0, 2.0) / row_width
    inverse = jnp.concatenate(
        [jnp.cos(angles).T * scaling[:, None], jnp.sin(angles).T * scaling[:, None]], axis=0
    ).astype(jnp.bfloat16)
    return (forward, inverse, frequency.astype(jnp.float32))


def rotate(spectrum, shifts, frequency, row_width):
    half_width = row_width // 2
    cosine_part = spectrum[..., :half_width]
    sine_part = spectrum[..., half_width:]
    angles = 2.0 * math.pi / row_width * frequency[None, :] * shifts[:, None]
    turn_cos = jnp.cos(angles)
    turn_sin = jnp.sin(angles)
    real_part = cosine_part * turn_cos - sine_part * turn_sin
    imag_part = cosine_part * turn_sin + sine_part * turn_cos
    return jnp.concatenate([real_part, imag_part], axis=-1).astype(jnp.bfloat16)


def fourier_shift(planes, shifts, forward, inverse, frequency, row_width):
    spectrum = jnp.einsum("bnw,wf->bnf", planes, forward, preferred_element_type=jnp.float32)
    rotated = rotate(spectrum, shifts, frequency, row_width)
    return jnp.einsum("bnf,fw->bnw", rotated, inverse, preferred_element_type=jnp.float32).astype(
        jnp.bfloat16
    )


def on_device(
    radiance,
    response,
    reference_tiles,
    chip_owner,
    tile_slot,
    row_offset,
    column_offset,
    valid_rows,
):
    owners = lax.axis_size("rows")
    device = lax.axis_index("rows")
    height = radiance.shape[1]
    row_width = radiance.shape[2]
    rim_rows = MAXDY + 1
    across = 2 * row_width // CHIP - 1
    capacity = max(2, (across + owners - 1) // owners)
    per_chip = CHIP // height
    first_row = device * height
    row_numbers = first_row + jnp.arange(height, dtype=jnp.int32)
    keep_rows = row_numbers < valid_rows[0]
    masked = radiance * keep_rows.astype(jnp.bfloat16)[None, :, None]
    band_partial = jnp.einsum("b,brw->rw", response, masked, preferred_element_type=jnp.float32)
    synthetic = lax.psum(band_partial.astype(jnp.bfloat16), "bands").astype(jnp.float32)
    chip_row = device // per_chip
    start_chip = chip_row * across
    owner_of = lax.dynamic_slice_in_dim(chip_owner[:, 0], start_chip, across)
    slot_of = lax.dynamic_slice_in_dim(tile_slot, start_chip, across)
    order_index = jnp.arange(across, dtype=jnp.int32)
    earlier = (owner_of[None, :] == owner_of[:, None]) & (
        order_index[None, :] < order_index[:, None]
    )
    rank_of = jnp.sum(earlier.astype(jnp.int32), axis=1)
    owner_index = jnp.arange(owners, dtype=jnp.int32)
    slot_index = jnp.arange(capacity, dtype=jnp.int32)
    route = (
        (owner_of[None, None, :] == owner_index[:, None, None])
        & (rank_of[None, None, :] == slot_index[None, :, None])
    ).astype(jnp.float32)
    choose = (
        slot_of[:, None] == jnp.arange(reference_tiles.shape[0], dtype=jnp.int32)[None, :]
    ).astype(jnp.float32)
    selector = jnp.einsum("osj,jt->ost", route, choose, precision=highest)
    window = hann_at(jnp.arange(CHIP, dtype=jnp.float32), CHIP)
    window_square = window[:, None] * window[None, :]
    chip_positions = (device % per_chip * height + jnp.arange(height, dtype=jnp.int32)).astype(
        jnp.float32
    )
    row_window = hann_at(chip_positions, CHIP)
    halves = synthetic.reshape(height, 2 * row_width // CHIP, CHIP // 2)
    cells = jnp.concatenate([halves[:, :-1], halves[:, 1:]], axis=-1)
    windowed = cells * (row_window[:, None, None] * window[None, None, :])
    cosine_table, sine_table = chip_tables(CHIP)
    tile_real, tile_imag = forward_spectra(
        reference_tiles * window_square, cosine_table, sine_table
    )
    forward_chip = jnp.concatenate([cosine_table, -sine_table], axis=1)
    column_spectra = jnp.einsum("rjc,cf->rjf", windowed, forward_chip, precision=highest)
    payload = jnp.einsum("osj,rjf->osrf", route, column_spectra, precision=highest)
    cell_rows = lax.all_to_all(
        payload.astype(jnp.bfloat16), "rows", split_axis=0, concat_axis=0, tiled=True
    ).astype(payload.dtype)
    tile_picks = lax.all_to_all(
        selector.astype(jnp.bfloat16), "rows", split_axis=0, concat_axis=0, tiled=True
    ).astype(selector.dtype)
    chip_cells = assemble(cell_rows, per_chip)
    chip_picks = first_of_chip(tile_picks, per_chip)
    back_real, back_imag = correlate_on_owner(
        chip_cells[..., :CHIP],
        chip_cells[..., CHIP:],
        chip_picks,
        tile_real,
        tile_imag,
        cosine_table,
        sine_table,
    )
    stacked = jnp.concatenate([back_real, back_imag], axis=-1)
    returned = lax.all_to_all(
        for_sending(split_rows(stacked, per_chip)), "rows", split_axis=0, concat_axis=0, tiled=True
    )
    gathered = jnp.einsum("osj,osrf->rjf", route, returned, precision=highest)
    surface_rows = jnp.einsum(
        "rjq,qv->rjv", gathered[..., :CHIP], cosine_table, precision=highest
    ) - jnp.einsum("rjq,qv->rjv", gathered[..., CHIP:], sine_table, precision=highest)
    surface_rows = surface_rows / float(CHIP) ** 3
    surface = surface_rows.reshape(height, across * CHIP)
    forward, inverse, frequency = shift_tables(row_width)
    own_fields = offset_fields(
        row_offset, column_offset, across, first_row.astype(jnp.float32), height
    )
    shifted = fourier_shift(masked, own_fields[:, 1], forward, inverse, frequency, row_width)
    extended = extended_2(shifted, (("rows", 1),), rim_rows)
    positions = first_row.astype(jnp.float32) + jnp.arange(height, dtype=jnp.float32)
    sources = positions - own_fields[:, 0]
    neighbours = (first_row - rim_rows).astype(jnp.float32) + jnp.arange(
        height + 2 * rim_rows, dtype=jnp.float32
    )
    resample = keys_kernel(neighbours[None, :] - sources[:, None]).astype(jnp.bfloat16)
    resampled = jnp.einsum("rq,bqw->brw", resample, extended, preferred_element_type=jnp.float32)
    aligned = (resampled * keep_rows.astype(jnp.float32)[None, :, None]).astype(jnp.bfloat16)
    return (aligned, surface)


def solution(mesh):
    return jax.shard_map(
        on_device,
        mesh=mesh,
        in_specs=(
            P("bands", ("groups", "rows"), None),
            P("bands"),
            P(("groups", "rows"), None, None),
            P("groups", None),
            P("groups"),
            P("groups"),
            P("groups"),
            P("groups"),
        ),
        out_specs=(P("bands", ("groups", "rows"), None), P(("groups", "rows"), None)),
        check_vma=False,
    )
```

profile of v0, /device:TPU:0, one launch (start us, length us, event | category | flops | bytes accessed | tf_op | source)
XLA Modules:
  0.0 139.2 jit_solution(15400113761500124256)
XLA Ops:
  7.9 3.6 %broadcast_multiply_fusion = bf16[112,32,1024]{2,1,0:T(8,128)(2,1)S(1)} fusion(bf16[112,32,1024]{2,1,0:T(8,128)(2,1)} %param.8, bf16[32]{0:T(256)(128)(2,1)S(1)} %compare_convert_fusion.1), kind=kLoop, calls=%fused_computation.16 | loop fusion | flops 3670016 | bytes 14680128 | tf_op jit(solution)/shard_map/mul | solution.py:181
  11.6 4.1 %fusion.9 = bf16[1,32,1024]{2,0,1:T(2,128)(2,1)S(1)} fusion(bf16[112,32,1024]{2,1,0:T(8,128)(2,1)S(1)} %broadcast_multiply_fusion, bf16[112]{0:T(256)(128)(2,1)S(1)} %copy-done), kind=kOutput, calls=%fused_computation.10 | convolution fusion | flops 7340032 | bytes 7405792 | tf_op jit(solution)/shard_map/b,brw->rw/dot_general | solution.py:182
  15.7 0.8 reshape.270
  17.0 0.7 copy.134
  17.8 7.3 %all-to-all-start.1 = ((bf16[8,2,2]{2,1,0:T(2,128)(2,1)}), bf16[8,2,2]{2,1,0:T(2,128)(2,1)S(1)}, u32[]{:S(2)}, u32[]{:S(2)}) async-start(bf16[8,2,2]{2,1,0:T(2,128)(2,1)} %copy.134), calls=%async_computation.1 | async-start | bytes 8192 | tf_op jit(solution)/shard_map/all_to_all | solution.py:222
  25.1 9.2 %sine_convert_fusion = (bf16[1024,512]{1,0:T(8,128)(2,1)}, bf16[1024,512]{1,0:T(8,128)(2,1)}) fusion(), kind=kLoop, calls=%fused_computation.40 | loop fusion | flops 8388608 | bytes 2097152 | tf_op jit(solution)/shard_map/convert.14
  34.3 0.6 fusion.233
  35.2 1.3 maximum_minimum_fusion
  36.7 9.6 %multiply_convert_fusion.2 = (bf16[512,1024]{1,0:T(8,128)(2,1)}, bf16[512,1024]{1,0:T(8,128)(2,1)}) fusion(f32[512]{0:T(512)S(1)} %select_multiply_fusion), kind=kLoop, calls=%fused_computation.37 | loop fusion | flops 9437184 | bytes 2099200 | tf_op jit(solution)/shard_map/convert.9
  46.3 0.3 multiply_cosine_fusion
  46.6 10.9 %fusion.23 = f32[112,32,1024]{2,1,0:T(8,128)S(1)} fusion(bf16[112,32,1024]{2,1,0:T(8,128)(2,1)} %copy-done.2, bf16[1024,512]{1,0:T(8,128)(2,1)} %get-tuple-element.24, bf16[1024,512]{1,0:T(8,128)(2,1)} %get-tuple-element.25), kind=kOutput, calls=%fused_computation.30 | convolution fusion | flops 7520387072 | bytes 24117248 | tf_op jit(solution)/shard_map/bnw,wf->bnf/dot_general | solution.py:153
  57.5 2.4 %subtract_convert_fusion = (bf16[112,32,512]{2,1,0:T(8,128)(2,1)S(1)}, bf16[112,32,512]{2,1,0:T(8,128)(2,1)S(1)}) fusion(f32[112,32,1024]{2,1,0:T(8,128)S(1)} %fusion.23, f32[32,512]{1,0:T(8,128)S(1)} %get-tuple-element.17, f32[32,512]{1,0:T(8,128)S(1)} %get-tuple-element.16), kind=kLoop, calls=%fused_computation.13 | loop fusion | flops 14680064 | bytes 22151168 | tf_op jit(solution)/shard_map/convert.11
  59.9 9.6 %fusion.11 = bf16[112,32,1024]{2,1,0:T(8,128)(2,1)S(1)} fusion(bf16[112,32,512]{2,1,0:T(8,128)(2,1)S(1)} %get-tuple-element.3, bf16[112,32,512]{2,1,0:T(8,128)(2,1)S(1)} %get-tuple-element.2, bf16[512,1024]{1,0:T(8,128)(2,1)} %get-tuple-element.19, bf16[512,1024]{1,0:T(8,128)(2,1)} %get-tuple-element.18), kind=kOutput, calls=%fused_computation.14 | convolution fusion | flops 7538737152 | bytes 16777216 | tf_op jit(solution)/shard_map/bnf,fw->bnw/dot_general | solution.py:155
  69.5 0.9 fusion.229
  70.6 4.2 %collective-permute-start = (bf16[112,3,1024]{2,0,1:T(8,128)(2,1)S(1)}, bf16[112,3,1024]{2,0,1:T(8,128)(2,1)S(1)}, u32[]{:S(2)}, u32[]{:S(2)}) collective-permute-start(bf16[112,3,1024]{2,0,1:T(8,128)(2,1)S(1)} %copy.124), channel_id=1, source_target_pairs={{0,2},{2,4},{4,6},{6,8},{8,10},{10,12},{12,14},{1,3},{3,5},{5,7},{... | collective-permute-start | bytes 2064392 | tf_op jit(solution)/shard_map/ppermute | solution.py:24
  75.1 1.3 collective-permute-start.1
  76.9 0.5 fusion.57
  77.4 0.5 convolution_negate_fusion
  78.1 0.5 fusion.85
  78.6 0.6 fusion.83
  79.2 0.6 fusion.41
  79.8 0.5 fusion.40
  80.5 1.0 fusion.232
  81.7 0.5 fusion.48
  82.3 0.6 convolution_convert_fusion
  82.9 0.8 copy.130
  83.7 7.4 %all-to-all-start = ((bf16[8,2,32,256]{3,2,1,0:T(8,128)(2,1)}), bf16[8,2,32,256]{3,2,1,0:T(8,128)(2,1)S(1)}, u32[]{:S(2)}, u32[]{:S(2)}) async-start(bf16[8,2,32,256]{3,2,1,0:T(8,128)(2,1)} %copy.130), calls=%async_computation | async-start | bytes 524288 | tf_op jit(solution)/shard_map/all_to_all | solution.py:219
  91.1 0.4 fusion.54
  91.7 0.4 fusion.52
  92.3 14.1 %all-to-all-done = bf16[8,2,32,256]{3,2,1,0:T(8,128)(2,1)S(1)} async-done(((bf16[8,2,32,256]{3,2,1,0:T(8,128)(2,1)}), bf16[8,2,32,256]{3,2,1,0:T(8,128)(2,1)S(1)}, u32[]{:S(2)}, u32[]{:S(2)}) %all-to-all-start) | async-done | bytes 262176 | tf_op jit(solution)/shard_map/all_to_all | solution.py:219
  106.4 0.5 fusion.62
  106.9 0.5 fusion.60
  107.5 0.6 fusion.37
  108.0 0.6 multiply_add_fusion
  108.6 0.6 fusion.74
  109.2 0.6 fusion.72
  109.9 0.6 fusion.35
  110.5 0.6 fusion.34
  111.1 0.3 fusion.231
  112.0 1.0 copy.151
  113.0 6.4 %all-to-all-start.2 = ((bf16[8,2,32,256]{3,1,2,0:T(2,128)(2,1)}), bf16[8,2,32,256]{3,1,2,0:T(2,128)(2,1)S(1)}, u32[]{:S(2)}, u32[]{:S(2)}) async-start(bf16[8,2,32,256]{3,1,2,0:T(2,128)(2,1)} %copy.151), calls=%async_computation.2 | async-start | bytes 524288 | tf_op jit(solution)/shard_map/all_to_all | solution.py:237
  119.3 0.6 copy.126
  120.0 1.7 %copy.127 = bf16[112,3,1024]{2,1,0:T(4,128)(2,1)S(1)} copy(bf16[112,3,1024]{2,0,1:T(8,128)(2,1)} %collective-permute-done.1) | data formatting | bytes 1376256 | tf_op jit(solution)/shard_map/ppermute | solution.py:27
  121.7 8.4 %fusion.14 = bf16[112,32,1024]{2,1,0:T(8,128)(2,1)} fusion(f32[32]{0:T(128)S(1)} %compare_convert_fusion, bf16[112,3,1024]{2,1,0:T(4,128)(2,1)S(1)} %copy.127, bf16[112,32,1024]{2,1,0:T(8,128)(2,1)} %copy-done.4, bf16[112,3,1024]{2,1,0:T(4,128)(2,1)S(1)} %copy.126, f32[32]{0:T(128)S(1)} %get-tuple-element.20, f32[38]{0:T(128)S(1)} %iota_add_fusion), kind=kOutput, calls=%fused_computation.15 | convolution fusion | flops 312432000 | bytes 16056728 | tf_op jit(solution)/shard_map/rq,bqw->brw/dot_general | solution.py:258
  130.1 0.3 convolution_bitcast_fusion
  130.4 0.6 fusion.46
  131.0 0.6 fusion.39
  131.7 0.7 copy.188
  (63 shorter events, 3.5 us)
Async XLA Ops:
  7.2 4.4 %copy-start = (bf16[112]{0:T(256)(128)(2,1)S(1)}, bf16[112]{0:T(256)(128)(2,1)}, u32[]{:S(2)}) copy-start(bf16[112]{0:T(256)(128)(2,1)} %param.9) | copy-start | bytes 676
  7.2 73.3 %all-reduce.2.cloned.1.call-start = ((), (), s32[]{:S(2)}) async-start(), calls=%async_computation.3 | async-start | bytes 262144 | tf_op jit(solution)/shard_map/psum | solution.py:183
  11.5 4.1 %copy-start.2 = (bf16[112,32,1024]{2,1,0:T(8,128)(2,1)}, bf16[112,32,1024]{2,1,0:T(8,128)(2,1)S(1)}, u32[]{:S(2)}) copy-start(bf16[112,32,1024]{2,1,0:T(8,128)(2,1)S(1)} %broadcast_multiply_fusion) | copy-start | bytes 22020100
  11.5 5.0 %copy-start.5 = (s32[30,1]{0,1:T(1,128)S(1)}, s32[30,1]{0,1:T(1,128)}, u32[]{:S(2)}) copy-start(s32[30,1]{0,1:T(1,128)} %param.11) | copy-start | bytes 364
  11.6 5.3 %copy-start.6 = (s32[30]{0:T(128)S(1)}, s32[30]{0:T(128)}, u32[]{:S(2)}) copy-start(s32[30]{0:T(128)} %param.12) | copy-start | bytes 364
  11.6 23.4 %copy-start.7 = (s32[30]{0:T(128)S(1)}, s32[30]{0:T(128)}, u32[]{:S(2)}) copy-start(s32[30]{0:T(128)} %param.14) | copy-start | bytes 364
  11.6 23.4 %copy-start.8 = (s32[30]{0:T(128)S(1)}, s32[30]{0:T(128)}, u32[]{:S(2)}) copy-start(s32[30]{0:T(128)} %param.13) | copy-start | bytes 364
  17.8 65.9 %all-to-all-start.1 = ((bf16[8,2,2]{2,1,0:T(2,128)(2,1)}), bf16[8,2,2]{2,1,0:T(2,128)(2,1)S(1)}, u32[]{:S(2)}, u32[]{:S(2)}) async-start(bf16[8,2,2]{2,1,0:T(2,128)(2,1)} %copy.134), calls=%async_computation.1 | async-start | bytes 8192 | tf_op jit(solution)/shard_map/all_to_all | solution.py:222
  69.5 5.6 %copy-start.4 = (bf16[112,32,1024]{2,1,0:T(8,128)(2,1)}, bf16[112,32,1024]{2,1,0:T(8,128)(2,1)S(1)}, u32[]{:S(2)}) copy-start(bf16[112,32,1024]{2,1,0:T(8,128)(2,1)S(1)} %fusion.11) | copy-start | bytes 22020100
  69.5 7.4 %copy-start.3 = (f32[2,128,128]{2,1,0:T(8,128)S(1)}, f32[2,128,128]{2,1,0:T(8,128)}, u32[]{:S(2)}) copy-start(f32[2,128,128]{2,1,0:T(8,128)} %param.10) | copy-start | bytes 393220
  70.6 48.7 %collective-permute-start = (bf16[112,3,1024]{2,0,1:T(8,128)(2,1)S(1)}, bf16[112,3,1024]{2,0,1:T(8,128)(2,1)S(1)}, u32[]{:S(2)}, u32[]{:S(2)}) collective-permute-start(bf16[112,3,1024]{2,0,1:T(8,128)(2,1)S(1)} %copy.124), channel_id=1, source_target_pairs={{0,2},{2,4},{4,6},{6,8},{8,10},{10,12},{12,14},{1,3},{3,5},{5,7},{... | collective-permute-start | bytes 2064392 | tf_op jit(solution)/shard_map/ppermute | solution.py:24
  75.1 44.8 %collective-permute-start.1 = (bf16[112,3,1024]{2,0,1:T(8,128)(2,1)S(1)}, bf16[112,3,1024]{2,0,1:T(8,128)(2,1)}, u32[]{:S(2)}, u32[]{:S(2)}) collective-permute-start(bf16[112,3,1024]{2,0,1:T(8,128)(2,1)S(1)} %copy.125), channel_id=1, source_target_pairs={{2,0},{4,2},{6,4},{8,6},{10,8},{12,10},{14,12},{3,1},{5,3},{7,5},{... | collective-permute-start | bytes 2064392 | tf_op jit(solution)/shard_map/ppermute | solution.py:27
  83.7 22.7 %all-to-all-start = ((bf16[8,2,32,256]{3,2,1,0:T(8,128)(2,1)}), bf16[8,2,32,256]{3,2,1,0:T(8,128)(2,1)S(1)}, u32[]{:S(2)}, u32[]{:S(2)}) async-start(bf16[8,2,32,256]{3,2,1,0:T(8,128)(2,1)} %copy.130), calls=%async_computation | async-start | bytes 524288 | tf_op jit(solution)/shard_map/all_to_all | solution.py:219
  113.0 17.1 %all-to-all-start.2 = ((bf16[8,2,32,256]{3,1,2,0:T(2,128)(2,1)}), bf16[8,2,32,256]{3,1,2,0:T(2,128)(2,1)S(1)}, u32[]{:S(2)}, u32[]{:S(2)}) async-start(bf16[8,2,32,256]{3,1,2,0:T(2,128)(2,1)} %copy.151), calls=%async_computation.2 | async-start | bytes 524288 | tf_op jit(solution)/shard_map/all_to_all | solution.py:237
  121.6 10.7 %copy-start.1 = (bf16[112]{0:T(256)(128)(2,1)S(1)}, bf16[112]{0:T(256)(128)(2,1)}, u32[]{:S(2)}) copy-start(bf16[112]{0:T(256)(128)(2,1)} %param.9) | copy-start | bytes 676
Sparse Core Ops, SparseCore 0:
  16.6 20.7 all-reduce.1
where the time goes:
time: 140 us; the launch traced here: 139 us
  matrix products  44.7 us (32%)
  other arithmetic  27.5 us (20%)
  starting transfers between devices  26.6 us (19%)
  between operations  15.2 us (11%)
  waiting for transfers between devices  14.1 us (10%)
  local copies, waits for them, and re-layouts  11.1 us (8%)
    another operation x4, other arithmetic  21.2 us
    all_to_all x1, waiting for transfers between devices, on_device(): lax.all_to_all(payload.astype(jnp.bfloat16), 'rows', split_axis=0, concat...  14.1 us
    dot_general x1, matrix products, fourier_shift(): jnp.einsum('bnw,wf->bnf', planes, forward, preferred_element_type=jnp.flo...  10.9 us
    dot_general x1, matrix products, fourier_shift(): jnp.einsum('bnf,fw->bnw', rotated, inverse, preferred_element_type=jnp.fl...  9.55 us
    dot_general x1, matrix products, on_device(): jnp.einsum('rq,bqw->brw', resample, extended, preferred_element_type=jnp....  8.42 us
    all_to_all x1, starting transfers between devices, on_device(): lax.all_to_all(payload.astype(jnp.bfloat16), 'rows', split_axis=0, concat...  7.43 us
    all_to_all x1, starting transfers between devices, on_device(): lax.all_to_all(selector.astype(jnp.bfloat16), 'rows', split_axis=0, conca...  7.31 us
    all_to_all x1, starting transfers between devices, on_device(): lax.all_to_all(for_sending(split_rows(stacked, per_chip)), 'rows', split_...  6.36 us
  transfers between devices with their start and end apart: 6, of which 1 were waited for; matrix products, arithmetic and copies ran while one was open for 52% of the time, Pallas kernels for 0%

commit v1 on v0

v1 whole, which is shorter than its diff:
```python
import functools
import math

import jax
import jax.numpy as jnp
import numpy as np
from jax import lax
from jax.experimental import pallas as pl
from jax.experimental.pallas import tpu as pltpu
from jax.sharding import PartitionSpec as P

CHIP = 128
MAXDY = 2
RIM = MAXDY + 1
GROUP = 16
PACK = 8

MESH = pl.DeviceIdType.MESH
bf16 = jnp.bfloat16
f32 = jnp.float32


def as_bf16(a):
    return np.asarray(a, np.float32).astype(jnp.bfloat16)


def split_np(a):
    a = np.asarray(a, np.float64)
    high = as_bf16(a)
    return high, as_bf16(a - high.astype(np.float64))


def shift_tables(width):
    half = width // 2
    samples = np.arange(half)
    tables = []
    for parity in (0, 1):
        freq = np.arange(parity, half, 2)
        angle = (np.outer(samples, freq) % width) * (2.0 * np.pi / width)
        forward = np.concatenate([np.cos(angle), np.sin(angle)], axis=1)
        scale = np.where(freq == 0, 1.0, 2.0)[:, None] / width
        inverse = np.concatenate([np.cos(angle).T * scale, np.sin(angle).T * scale], axis=0)
        tables += [as_bf16(forward), as_bf16(inverse)]
    return tables


def chip_tables():
    index = np.arange(CHIP)
    angle = (np.outer(index, index) % CHIP) * (2.0 * np.pi / CHIP)
    c, s = np.cos(angle), np.sin(angle)
    window = 0.5 - 0.5 * np.cos(index * (2.0 * np.pi / CHIP))
    columns = window[:, None] * np.concatenate([c, -s], axis=1)
    cw, sw = c * window, s * window
    rows = np.block([[cw, sw], [-sw, cw]])
    last = np.concatenate([c, -s], axis=0) / float(CHIP) ** 3
    return columns, rows, c, s, last


def dot(a, b):
    return jnp.dot(a, b, preferred_element_type=f32)


def split(a):
    high = a.astype(bf16)
    return high, (a - high.astype(f32)).astype(bf16)


def dot3(a, b):
    (ah, al), (bh, bl) = a, b
    return dot(ah, bh) + dot(ah, bl) + dot(al, bh)


def shift_rows(x, cos, sin, fe, ge, fo, go):
    rows, width = x.shape
    half, quarter = width // 2, width // 4
    period = cos.shape[0]
    lo, hi = x[:, :half], x[:, half:]

    def part(values, forward, inverse, first):
        spectrum = dot(values, forward)
        turn_c = cos[:, first : first + quarter][None]
        turn_s = sin[:, first : first + quarter][None]
        c = spectrum[:, :quarter].reshape(rows // period, period, quarter)
        s = spectrum[:, quarter:].reshape(rows // period, period, quarter)
        p = (c * turn_c - s * turn_s).reshape(rows, quarter).astype(bf16)
        q = (c * turn_s + s * turn_c).reshape(rows, quarter).astype(bf16)
        return dot(p, inverse[:quarter]) + dot(q, inverse[quarter:])

    even = part(lo + hi, fe[...], ge[...], 0)
    odd = part(lo - hi, fo[...], go[...], quarter)
    return (even + odd).astype(bf16), (even - odd).astype(bf16)


def shift_kernel(
    near,
    resp_ref, x_hbm, tiles_ref, keep_ref, cos_ref, sin_ref, fe, ge, fo, go,
    xs_hbm, syn_out, tiles_out,
    xbuf, obuf, partial, other, total, syn_buf, tile_buf,
    in_sem, out_sem, pair_sem, syn_send, syn_recv, tile_send, tile_recv,
):
    count = lax.axis_size("rows")
    me = lax.axis_index("rows")
    core = lax.axis_index("bands")
    steps, group, height, width = xbuf.shape
    in_copies = [
        pltpu.make_async_copy(x_hbm.at[pl.ds(g * group, group)], xbuf.at[g], in_sem.at[g])
        for g in range(steps)
    ]
    for copy in in_copies:
        copy.start()

    barrier = pltpu.get_barrier_semaphore()
    for d in range(1, count):
        pl.semaphore_signal(
            barrier, inc=1, device_id={"rows": lax.rem(me + d, count)}, device_id_type=MESH
        )
    pl.semaphore_signal(barrier, inc=1, device_id={"bands": 1 - core}, device_id_type=MESH)
    pl.semaphore_wait(barrier, count)

    tile_copies = []
    for d in range(1, count):
        copy = pltpu.make_async_remote_copy(
            src_ref=tiles_ref, dst_ref=tile_buf.at[d], send_sem=tile_send.at[d],
            recv_sem=tile_recv.at[d], device_id={"rows": lax.rem(me + d, count)},
            device_id_type=MESH,
        )
        copy.start()
        tile_copies.append(copy)

    acc = jnp.zeros((height, width), f32)
    for g in range(steps):
        in_copies[g].wait()

        def add(b, acc, g=g):
            return acc + resp_ref[g * group + b] * xbuf[g, b].astype(f32)

        acc = lax.fori_loop(0, group, add, acc)
    partial[...] = (acc * keep_ref[...]).astype(bf16)
    pair = pltpu.make_async_remote_copy(
        src_ref=partial, dst_ref=other, send_sem=pair_sem.at[0], recv_sem=pair_sem.at[1],
        device_id={"bands": 1 - core}, device_id_type=MESH,
    )
    pair.start()

    def out_copy(g):
        return pltpu.make_async_copy(
            obuf.at[g], xs_hbm.at[pl.ds(g * group * height, group * height)], out_sem.at[g]
        )

    def shift_step(g, carry):
        x = xbuf[g].reshape(group * height, width)
        left, right = shift_rows(x, cos_ref[...], sin_ref[...], fe, ge, fo, go)
        obuf[g, :, : width // 2] = left
        obuf[g, :, width // 2 :] = right
        out_copy(g).start()
        return carry

    first = min(2, steps)
    lax.fori_loop(0, first, shift_step, 0)
    pair.wait()
    total[...] = (partial[...].astype(f32) + other[...].astype(f32)).astype(bf16)
    base = me // near * near
    spot = lax.rem(me, near)
    syn_copies = []
    for d in range(1, near):
        copy = pltpu.make_async_remote_copy(
            src_ref=total, dst_ref=syn_buf.at[d], send_sem=syn_send.at[d],
            recv_sem=syn_recv.at[d], device_id={"rows": base + lax.rem(spot + d, near)},
            device_id_type=MESH,
        )
        copy.start()
        syn_copies.append(copy)
    lax.fori_loop(first, steps, shift_step, 0)

    syn_out[pl.ds(spot, 1)] = total[...][None]
    for d, copy in enumerate(syn_copies, 1):
        copy.wait()
        syn_out[pl.ds(lax.rem(spot + near - d, near), 1)] = syn_buf[d][None]
    tiles_out[pl.ds(me, 1)] = tiles_ref[...][None]
    for d, copy in enumerate(tile_copies, 1):
        copy.wait()
        tiles_out[pl.ds(lax.rem(me + count - d, count), 1)] = tile_buf[d][None]
    for g in range(steps):
        out_copy(g).wait()


def corr_kernel(
    index_ref, syn_ref, tiles_ref, colh, coll, rowh, rowl, backh, backl, lasth, lastl,
    out_ref, a_ref,
):
    syn = syn_ref[...]
    width = syn.shape[1]
    across = 2 * width // CHIP - 1
    rolled = pltpu.roll(syn.astype(f32), width - CHIP // 2, 1).astype(bf16)
    chips, tiles = [], []
    for j in range(across):
        source = rolled if j % 2 else syn
        chips.append(source[:, j // 2 * CHIP : (j // 2 + 1) * CHIP])
        tiles.append(tiles_ref[index_ref[j]])

    def spectra(blocks):
        stacked = jnp.concatenate(blocks, axis=0)
        column = dot(stacked, colh[...]) + dot(stacked, coll[...])
        for j in range(across):
            block = column[j * CHIP : (j + 1) * CHIP]
            a_ref[:CHIP, j * CHIP : (j + 1) * CHIP] = block[:, :CHIP]
            a_ref[CHIP:, j * CHIP : (j + 1) * CHIP] = block[:, CHIP:]
        return dot3((rowh[...], rowl[...]), split(a_ref[...]))

    x = spectra(chips)
    y = spectra(tiles)
    xr, xi, yr, yi = x[:CHIP], x[CHIP:], y[:CHIP], y[CHIP:]
    a_ref[:CHIP] = xr * yr + xi * yi
    a_ref[CHIP:] = xi * yr - xr * yi
    spot = index_ref[across]
    back = dot3((backh[spot], backl[spot]), split(a_ref[...]))
    height = back.shape[0] // 2
    rows = jnp.concatenate(
        [
            jnp.concatenate(
                [
                    back[:height, j * CHIP : (j + 1) * CHIP],
                    back[height:, j * CHIP : (j + 1) * CHIP],
                ],
                axis=1,
            )
            for j in range(across)
        ],
        axis=0,
    )
    surface = dot3(split(rows), (lasth[...], lastl[...]))
    for j in range(across):
        out_ref[:, j * CHIP : (j + 1) * CHIP] = surface[j * height : (j + 1) * height]


def resample_kernel(
    xs_ref, low_ref, high_ref, cos_ref, sin_ref, fe, ge, fo, go, inner_ref, rim_ref,
    out_ref, halo,
):
    width = xs_ref.shape[1]
    half = width // 2

    @pl.when(pl.program_id(0) == 0)
    def _():
        steps = halo.shape[0]
        for side, ref in enumerate((low_ref, high_ref)):
            left, right = shift_rows(ref[...], cos_ref[side], sin_ref[side], fe, ge, fo, go)
            size = ref.shape[0] // steps
            for g in range(steps):
                rows = slice(g * size, (g + 1) * size)
                halo[g, side * size : (side + 1) * size, :half] = left[rows]
                halo[g, side * size : (side + 1) * size, half:] = right[rows]

    rim = halo[pl.program_id(0)]
    size = inner_ref.shape[0]
    for s in range(GROUP // PACK):
        rows = slice(s * size, (s + 1) * size)
        out_ref[rows] = (dot(inner_ref[...], xs_ref[rows]) + dot(rim_ref[s], rim)).astype(bf16)


def keys_kernel(distance):
    magnitude = jnp.abs(distance)
    inner_part = (1.5 * magnitude - 2.5) * magnitude * magnitude + 1.0
    outer_part = ((-0.5 * magnitude + 2.5) * magnitude - 4.0) * magnitude + 2.0
    return jnp.where(magnitude <= 1.0, inner_part, jnp.where(magnitude < 2.0, outer_part, 0.0))


def offset_fields(row_offset, column_offset, across, first_row, row_count):
    chip_rows = row_offset.shape[0] // across
    scale = 64.0 * across
    row_means = jnp.sum(row_offset.astype(f32).reshape(chip_rows, across), axis=1) / scale
    column_means = jnp.sum(column_offset.astype(f32).reshape(chip_rows, across), axis=1) / scale
    centres = jnp.arange(chip_rows, dtype=f32) * CHIP + (CHIP - 1) * 0.5
    positions = first_row + jnp.arange(row_count, dtype=f32)
    clipped = jnp.clip(positions, (CHIP - 1) * 0.5, (chip_rows - 1) * CHIP + (CHIP - 1) * 0.5)
    weights = jnp.maximum(1.0 - jnp.abs(clipped[:, None] - centres[None, :]) / CHIP, 0.0)
    return (
        jnp.sum(weights * row_means[None], axis=1),
        jnp.sum(weights * column_means[None], axis=1),
    )


def on_device(
    radiance, response, reference_tiles, chip_owner, tile_slot, row_offset, column_offset,
    valid_rows,
):
    count = lax.axis_size("rows")
    device = lax.axis_index("rows")
    bands, height, width = radiance.shape
    tile_count = reference_tiles.shape[0]
    half = width // 2
    across = 2 * width // CHIP - 1
    near = CHIP // height
    first_row = device * height
    steps = bands // GROUP

    forward = [(i, i + 1) for i in range(count - 1)]
    backward = [(i + 1, i) for i in range(count - 1)]
    low = lax.ppermute(radiance[:, height - RIM :].reshape(bands * RIM, width), "rows", forward)
    high = lax.ppermute(radiance[:, :RIM].reshape(bands * RIM, width), "rows", backward)

    tables = shift_tables(width)
    columns, rows, chip_c, chip_s, last = chip_tables()

    outer = height + 2 * RIM
    row_shift, column_shift = offset_fields(
        row_offset, column_offset, across, (first_row - RIM).astype(f32), outer
    )
    numbers = first_row - RIM + jnp.arange(outer, dtype=jnp.int32)
    keep = (numbers < valid_rows[0]).astype(f32)
    frequency = np.concatenate([np.arange(0, half, 2), np.arange(1, half, 2)]).astype(np.float32)
    angles = (2.0 * math.pi / width) * frequency[None, :] * column_shift[:, None]
    turn_cos = jnp.cos(angles) * keep[:, None]
    turn_sin = jnp.sin(angles) * keep[:, None]
    own = slice(RIM, RIM + height)

    def rim_turn(turn):
        sides = jnp.stack([turn[:RIM], turn[RIM + height :]])
        return jnp.tile(sides, (1, GROUP, 1))

    keep_own = keep[own]
    shift_own = row_shift[own]

    vmem = pl.BlockSpec(memory_space=pltpu.VMEM)
    smem = pl.BlockSpec(memory_space=pltpu.SMEM)
    anywhere = pl.BlockSpec(memory_space=pl.ANY)
    dma = pltpu.SemaphoreType.DMA
    flops = 8 * bands * height * half * half
    xs, syn_all, tiles_all = pl.pallas_call(
        functools.partial(shift_kernel, near),
        out_shape=(
            jax.ShapeDtypeStruct((bands * height, width), bf16),
            jax.ShapeDtypeStruct((near, height, width), bf16),
            jax.ShapeDtypeStruct((count, tile_count, CHIP, CHIP), bf16),
        ),
        in_specs=[smem, anywhere] + [vmem] * 8,
        out_specs=(anywhere, vmem, vmem),
        scratch_shapes=[
            pltpu.VMEM((steps, GROUP, height, width), bf16),
            pltpu.VMEM((steps, GROUP * height, width), bf16),
            pltpu.VMEM((height, width), bf16),
            pltpu.VMEM((height, width), bf16),
            pltpu.VMEM((height, width), bf16),
            pltpu.VMEM((near, height, width), bf16),
            pltpu.VMEM((count, tile_count, CHIP, CHIP), bf16),
            dma((steps,)), dma((steps,)), dma((2,)),
            dma((near,)), dma((near,)), dma((count,)), dma((count,)),
        ],
        compiler_params=pltpu.CompilerParams(collective_id=0, has_side_effects=True),
        cost_estimate=pl.CostEstimate(
            flops=flops, bytes_accessed=4 * bands * height * width, transcendentals=0
        ),
        name="shift",
    )(
        response.astype(f32), radiance, reference_tiles.astype(bf16),
        jnp.broadcast_to(keep_own[:, None], (height, width)),
        turn_cos[own], turn_sin[own], *tables,
    )

    chip_row = device // near
    owner_of = lax.dynamic_slice_in_dim(chip_owner[:, 0], chip_row * across, across)
    slot_of = lax.dynamic_slice_in_dim(tile_slot, chip_row * across, across)
    index = jnp.concatenate(
        [owner_of * tile_count + slot_of, jnp.full((1,), device % near, jnp.int32)]
    )
    back = np.stack(
        [
            np.block([[chip_c[u], -chip_s[u]], [chip_s[u], chip_c[u]]])
            for u in (slice(i * height, (i + 1) * height) for i in range(near))
        ]
    )
    surface = pl.pallas_call(
        corr_kernel,
        out_shape=jax.ShapeDtypeStruct((height, across * CHIP), f32),
        in_specs=[smem] + [vmem] * 10,
        out_specs=vmem,
        scratch_shapes=[pltpu.VMEM((2 * CHIP, across * CHIP), f32)],
        cost_estimate=pl.CostEstimate(
            flops=2_500_000_000, bytes_accessed=4_000_000, transcendentals=0
        ),
        name="correlate",
    )(
        index, syn_all.reshape(near * height, width),
        tiles_all.reshape(count * tile_count, CHIP, CHIP),
        *split_np(columns), *split_np(rows), *split_np(back), *split_np(last),
    )

    size = PACK * height
    row_of = np.arange(size) % height
    band_of = np.arange(size) // height
    source = np.arange(height, dtype=np.float32)
    place = jnp.tile(source - shift_own, PACK)[:, None]
    keep_rows = jnp.tile(keep_own, PACK)[:, None]
    same = (band_of[:, None] == band_of[None, :]).astype(np.float32)
    inner = (keys_kernel(row_of[None, :].astype(np.float32) - place) * (same * keep_rows)).astype(bf16)
    rim_band = np.tile(np.repeat(np.arange(GROUP), RIM), 2)
    rim_row = np.concatenate(
        [np.tile(np.arange(RIM) - RIM, GROUP), np.tile(np.arange(RIM) + height, GROUP)]
    ).astype(np.float32)
    joined = np.stack(
        [
            (band_of[:, None] + s * PACK == rim_band[None, :]).astype(np.float32)
            for s in range(GROUP // PACK)
        ]
    )
    rim = ((keys_kernel(rim_row[None, :] - place) * keep_rows)[None] * joined).astype(bf16)

    block = pl.BlockSpec((GROUP * height, width), lambda g: (g, 0))
    aligned = pl.pallas_call(
        resample_kernel,
        grid=(steps,),
        out_shape=jax.ShapeDtypeStruct((bands * height, width), bf16),
        in_specs=[block] + [vmem] * 10,
        out_specs=block,
        scratch_shapes=[pltpu.VMEM((steps, 2 * RIM * GROUP, width), bf16)],
        compiler_params=pltpu.CompilerParams(dimension_semantics=("arbitrary",)),
        cost_estimate=pl.CostEstimate(
            flops=3_000_000_000, bytes_accessed=4 * bands * height * width, transcendentals=0
        ),
        name="resample",
    )(xs, low, high, rim_turn(turn_cos), rim_turn(turn_sin), *tables, inner, rim)
    return (aligned.reshape(bands, height, width), surface)


def solution(mesh):
    return jax.shard_map(
        on_device,
        mesh=mesh,
        in_specs=(
            P("bands", ("groups", "rows"), None),
            P("bands"),
            P(("groups", "rows"), None, None),
            P("groups", None),
            P("groups"),
            P("groups"),
            P("groups"),
            P("groups"),
        ),
        out_specs=(P("bands", ("groups", "rows"), None), P(("groups", "rows"), None)),
        check_vma=False,
    )
```

time: 140 us -> 71.3 us (0.51)
  Pallas kernels: 0 us -> 45.9 us
  matrix products: 44.7 us -> 0 us
  starting transfers between devices: 26.6 us -> 6.23 us
  other arithmetic: 27.5 us -> 7.27 us
  waiting for transfers between devices: 14.1 us -> 0.01 us
  between operations: 15.2 us -> 1.48 us
  local copies, waits for them, and re-layouts: 11.1 us -> 9.4 us
    pallas_call x0 -> x3, Pallas kernels: none -> 45.9 us  [the longest x1 26 us: on_device(): pl.pallas_call(functools.partial(shift_kernel, near), out_shape=(jax.Shap...]
    dot_general x27 -> x0, matrix products: 44.7 us -> none  [the longest x1 10.9 us: fourier_shift(): jnp.einsum('bnw,wf->bnf', planes, forward, preferred_element_type=jnp.flo...]
    another operation x4 -> x2, other arithmetic: 21.2 us -> 0.01 us  [rim_turn(): sides = jnp.stack([turn[:RIM], turn[RIM + height:]])]
    all_to_all x3 -> x0, starting transfers between devices: 21.1 us -> none  [the longest x1 7.43 us: on_device(): lax.all_to_all(payload.astype(jnp.bfloat16), 'rows', split_axis=0, concat...]
    all_to_all x3 -> x0, waiting for transfers between devices: 14.1 us -> none  [the longest x1 14.1 us: on_device(): lax.all_to_all(payload.astype(jnp.bfloat16), 'rows', split_axis=0, concat...]
    convert_element_type x3 -> x7, other arithmetic: 0.05 us -> 5 us  [the longest x1 1.54 us: on_device(): reference_tiles.astype(bf16)]
    mul x5 -> x2, other arithmetic: 3.93 us -> 1.19 us  [the longest x1 1.05 us: on_device(): turn_sin = jnp.sin(angles) * keep[:, None]]
    convert_element_type x3 -> x0, local copies, waits for them, and re-layouts: 2.47 us -> none  [the longest x1 0.99 us: for_sending(): a.astype(jnp.bfloat16)]
  transfers between devices with their start and end apart: 6 -> 2, of which waited for: 1 -> 0; matrix products, arithmetic and copies ran while one was open for 52% -> 17% of each run, Pallas kernels for 0% -> 47%
where the time goes in v1:
time: 71.3 us; the launch traced here: 70.3 us
  Pallas kernels  45.9 us (64%)
  local copies, waits for them, and re-layouts  9.4 us (13%)
  other arithmetic  7.27 us (10%)
  starting transfers between devices  6.23 us (9%)
  between operations  1.48 us (2%)
    pallas_call x1, Pallas kernels, on_device(): pl.pallas_call(functools.partial(shift_kernel, near), out_shape=(jax.Shap...  26 us
    pallas_call x1, Pallas kernels, on_device(): pl.pallas_call(resample_kernel, grid=(steps,), out_shape=jax.ShapeDtypeSt...  12.9 us
    pallas_call x1, Pallas kernels, on_device(): pl.pallas_call(corr_kernel, out_shape=jax.ShapeDtypeStruct((height, acros...  6.92 us
    ppermute x1, starting transfers between devices, on_device(): lax.ppermute(radiance[:, height - RIM:].reshape(bands * RIM, width), 'row...  4.94 us
    slice x1, local copies, waits for them, and re-layouts, on_device(): radiance[:, :RIM].reshape(bands * RIM, width)  2.95 us
    another operation x4, local copies, waits for them, and re-layouts, rim_turn(): return jnp.tile(sides, (1, GROUP, 1))  1.57 us
    convert_element_type x1, other arithmetic, on_device(): reference_tiles.astype(bf16)  1.54 us
  transfers between devices with their start and end apart: 2, of which 0 were waited for; matrix products, arithmetic and copies ran while one was open for 17% of the time, Pallas kernels for 47%

profile of v1, /device:TPU:0, one launch (start us, length us, event | category | flops | bytes accessed | tf_op | source)
XLA Modules:
  0.0 70.3 jit_solution(2928689899508141167)
XLA Ops:
  0.6 0.0 copy-start.4
  0.6 0.0 copy-start.2
  0.7 0.0 copy-start.8
  0.7 0.0 copy-start.6
  0.7 0.0 copy-start.7
  0.7 3.0 %fusion.13 = (bf16[112,3,1024]{2,1,0:T(4,128)(2,1)S(1)}, bf16[112,3,1024]{2,1,0:T(4,128)(2,1)S(1)}) fusion(bf16[112,32,1024]{2,1,0:T(8,128)(2,1)} %x_hbm.1), kind=kLoop, calls=%fused_computation.37 | loop fusion | bytes 2752512 | tf_op jit(solution)/shard_map/slice | solution.py:300
  3.6 0.6 reshape.125
  4.3 4.9 %collective-permute-start = (bf16[336,1024]{1,0:T(8,128)(2,1)S(1)}, bf16[336,1024]{1,0:T(8,128)(2,1)S(1)}, u32[]{:S(2)}, u32[]{:S(2)}) collective-permute-start(bf16[336,1024]{1,0:T(8,128)(2,1)S(1)} %reshape.125), channel_id=1, source_target_pairs={{0,2},{2,4},{4,6},{6,8},{8,10},{10,12},{12,14},{1,3},{3,5},{5,7},{... | collective-permute-start | bytes 2064392 | tf_op jit(solution)/shard_map/ppermute | solution.py:299
  9.2 0.6 reshape.126
  9.8 1.3 %collective-permute-start.1 = (bf16[336,1024]{1,0:T(8,128)(2,1)S(1)}, bf16[336,1024]{1,0:T(8,128)(2,1)S(1)}, u32[]{:S(2)}, u32[]{:S(2)}) collective-permute-start(bf16[336,1024]{1,0:T(8,128)(2,1)S(1)} %reshape.126), channel_id=1, source_target_pairs={{2,0},{4,2},{6,4},{8,6},{10,8},{12,10},{14,12},{3,1},{5,3},{7,5},{... | collective-permute-start | bytes 2064392 | tf_op jit(solution)/shard_map/ppermute | solution.py:300
  11.8 0.1 slice.30
  11.9 0.7 convert_element_type.33
  12.6 0.1 reshape.127
  12.6 0.7 convert_element_type.32
  13.3 0.1 reshape.124
  13.4 0.1 reduce_sum.38
  13.5 0.1 reduce_sum.36
  13.6 0.1 multiply_reduce_fusion
  13.7 1.0 %fusion.12 = (f32[38,512]{1,0:T(8,128)S(1)}, f32[38,512]{1,0:T(8,128)S(1)}) fusion(f32[38]{0:T(128)S(1)} %compare_convert_fusion, f32[38]{0:T(128)S(1)} %get-tuple-element.9, f32[512]{0:T(512)} %constant.140), kind=kLoop, calls=%fused_computation.19 | loop fusion | flops 58368 | bytes 158000 | tf_op jit(solution)/shard_map/mul | solution.py:314
  14.8 0.6 slice.41.sin_ref
  15.4 0.6 slice.40.cos_ref
  16.1 0.0 copy-done.8
  16.1 0.6 convert_element_type.28.resp_ref
  16.6 0.1 slice_subtract_fusion
  16.7 0.1 sub.87
  16.8 0.1 mul.191
  16.9 1.5 %convert_element_type.29.tiles_ref = bf16[2,128,128]{2,1,0:T(8,128)(2,1)} convert(f32[2,128,128]{2,1,0:T(8,128)} %param.28) | non-fusion elementwise | flops 32768 | bytes 196608 | tf_op jit(solution)/shard_map/convert_element_type | solution.py:355
  18.5 0.1 tile.12
  18.5 0.7 %copy.34.cos_ref = f32[2,48,512]{2,1,0:T(8,128)} copy(f32[2,48,512]{2,0,1:T(2,128)S(1)} %bitcast.19) | data formatting | bytes 393216 | tf_op jit(solution)/shard_map/tile | solution.py:319
  19.3 0.1 tile.14
  19.3 0.7 %copy.35.sin_ref = f32[2,48,512]{2,1,0:T(8,128)} copy(f32[2,48,512]{2,0,1:T(2,128)S(1)} %bitcast.20) | data formatting | bytes 393216 | tf_op jit(solution)/shard_map/tile | solution.py:319
  20.1 0.0 copy-done.6
  20.1 0.1 bitcast_add_fusion
  20.1 0.6 pad_add_fusion.index_ref
  20.7 0.9 %fusion.3.inner_ref = bf16[256,256]{1,0:T(8,128)(2,1)} fusion(f32[256,256]{1,0:T(8,128)S(1)} %copy-done.2, f32[256]{0:T(256)S(1)} %mul.191, f32[256]{0:T(256)S(1)} %sub.87, f32[256]{0:T(256)S(1)} %copy-done.4), kind=kLoop, calls=%fused_computation.4 | loop fusion | flops 1310720 | bytes 396288 | tf_op jit(solution)/shard_map/convert_element_type | solution.py:395
  21.6 0.7 %broadcast_in_dim.10.keep_ref = f32[32,1024]{1,0:T(8,128)} broadcast(f32[32]{0:T(128)S(1)} %slice.30), dimensions={0} | broadcast | bytes 131200 | tf_op jit(solution)/shard_map/broadcast_in_dim | solution.py:356
  22.3 26.0 %shift.1 = (bf16[3584,1024]{1,0:T(8,128)(2,1)}, bf16[4,32,1024]{2,1,0:T(8,128)(2,1)}, bf16[8,2,128,128]{3,2,1,0:T(8,128)(2,1)}) custom-call(f32[112]{0:T(128)} %convert_element_type.28.resp_ref, bf16[112,32,1024]{2,1,0:T(8,128)(2,1)} %x_hbm.1, bf16[2,128,128]{2,1,0:T(8,128)(2,1)} %convert_element_type.29.tiles_ref, f32[32,1024]{1,0:T(8,128)} %broadcast_in_dim.10.keep_ref, ...), custom_call_target="tpu_custom_call" | custom-call | flops 7516192768 | bytes 14680064 | tf_op jit(solution)/shard_map/shift/pallas_call | solution.py:329
  48.4 0.0 copy-start.3
  48.4 0.1 fusion.8
  48.5 6.9 %correlate.1 = f32[32,1920]{1,0:T(8,128)} custom-call(s32[16]{0:T(128)} %pad_add_fusion.index_ref, bf16[128,1024]{1,0:T(8,128)(2,1)} %bitcast.22, bf16[16,128,128]{2,1,0:T(8,128)(2,1)} %bitcast.21, bf16[128,256]{1,0:T(8,128)(2,1)} %constant.126.clone.colh, bf16[128,256]{1,0:T(8,128)(2,1)} %constant.127.clone.coll, bf16[256,256]{1,0:T(8,128)(2,1)} %constant.128.clone.rowh, ...), custom_call_target="tpu_custom_call" | custom-call | flops 2500000000 | bytes 4000000 | tf_op jit(solution)/shard_map/correlate/pallas_call | solution.py:372
  55.5 0.0 copy-done.3
  55.5 0.7 multiply_convert_fusion.rim_ref
  56.2 0.0 collective-permute-done.low_ref
  56.2 0.0 collective-permute-done.1.high_ref
  56.2 0.0 copy-start.1
  56.2 0.8 %copy-done = bf16[336,1024]{1,0:T(8,128)(2,1)} copy-done((bf16[336,1024]{1,0:T(8,128)(2,1)}, bf16[336,1024]{1,0:T(8,128)(2,1)S(1)}, u32[]{:S(2)}) %copy-start) | copy-done | bytes 688152
  57.0 0.3 copy-done.1
  57.3 12.9 %resample.1 = bf16[3584,1024]{1,0:T(8,128)(2,1)} custom-call(bf16[3584,1024]{1,0:T(8,128)(2,1)} %get-tuple-element.5.xs_ref, bf16[336,1024]{1,0:T(8,128)(2,1)} %copy-done, bf16[336,1024]{1,0:T(8,128)(2,1)} %copy-done.1, f32[2,48,512]{2,1,0:T(8,128)} %copy.34.cos_ref, f32[2,48,512]{2,1,0:T(8,128)} %copy.35.sin_ref, bf16[512,512]{1,0:T(8,128)(2,1)} %constant.122.clone.fe, ...), custom_call_target="tpu_custom_call" | custom-call | flops 3000000000 | bytes 14680064 | tf_op jit(solution)/shard_map/resample/pallas_call | solution.py:409
  (18 shorter events, 0.1 us)
Async XLA Ops:
  0.6 20.1 %copy-start.4 = (f32[256]{0:T(256)S(1)}, f32[256]{0:T(256)}, u32[]{:S(2)}) copy-start(f32[256]{0:T(256)} %constant.141) | copy-start | bytes 3076
  0.6 20.1 %copy-start.2 = (f32[256,256]{1,0:T(8,128)S(1)}, f32[256,256]{1,0:T(8,128)}, u32[]{:S(2)}) copy-start(f32[256,256]{1,0:T(8,128)} %constant.135.clone) | copy-start | bytes 786436
  0.7 15.4 %copy-start.8 = (bf16[112]{0:T(256)(128)(2,1)S(1)}, bf16[112]{0:T(256)(128)(2,1)}, u32[]{:S(2)}) copy-start(bf16[112]{0:T(256)(128)(2,1)} %param.27) | copy-start | bytes 676
  0.7 19.4 %copy-start.6 = (s32[30]{0:T(128)S(1)}, s32[30]{0:T(128)}, u32[]{:S(2)}) copy-start(s32[30]{0:T(128)} %param.30) | copy-start | bytes 364
  0.7 19.4 %copy-start.7 = (s32[30,1]{0,1:T(1,128)S(1)}, s32[30,1]{0,1:T(1,128)}, u32[]{:S(2)}) copy-start(s32[30,1]{0,1:T(1,128)} %param.29) | copy-start | bytes 364
  4.3 51.9 %collective-permute-start = (bf16[336,1024]{1,0:T(8,128)(2,1)S(1)}, bf16[336,1024]{1,0:T(8,128)(2,1)S(1)}, u32[]{:S(2)}, u32[]{:S(2)}) collective-permute-start(bf16[336,1024]{1,0:T(8,128)(2,1)S(1)} %reshape.125), channel_id=1, source_target_pairs={{0,2},{2,4},{4,6},{6,8},{8,10},{10,12},{12,14},{1,3},{3,5},{5,7},{... | collective-permute-start | bytes 2064392 | tf_op jit(solution)/shard_map/ppermute | solution.py:299
  9.8 46.3 %collective-permute-start.1 = (bf16[336,1024]{1,0:T(8,128)(2,1)S(1)}, bf16[336,1024]{1,0:T(8,128)(2,1)S(1)}, u32[]{:S(2)}, u32[]{:S(2)}) collective-permute-start(bf16[336,1024]{1,0:T(8,128)(2,1)S(1)} %reshape.126), channel_id=1, source_target_pairs={{2,0},{4,2},{6,4},{8,6},{10,8},{12,10},{14,12},{3,1},{5,3},{7,5},{... | collective-permute-start | bytes 2064392 | tf_op jit(solution)/shard_map/ppermute | solution.py:300
  22.3 26.0 %copy-start.5 = (f32[96]{0:T(128)S(1)}, f32[96]{0:T(128)}, u32[]{:S(2)}) copy-start(f32[96]{0:T(128)} %constant.142) | copy-start | bytes 1156
  48.4 7.1 %copy-start.3 = (f32[2,256,96]{2,1,0:T(8,128)S(1)}, f32[2,256,96]{2,1,0:T(8,128)}, u32[]{:S(2)}) copy-start(f32[2,256,96]{2,1,0:T(8,128)} %constant.137.clone) | copy-start | bytes 589828
  56.2 0.8 %copy-start = (bf16[336,1024]{1,0:T(8,128)(2,1)}, bf16[336,1024]{1,0:T(8,128)(2,1)S(1)}, u32[]{:S(2)}) copy-start(bf16[336,1024]{1,0:T(8,128)(2,1)S(1)} %collective-permute-done.low_ref) | copy-start | bytes 2064388
  56.2 1.2 %copy-start.1 = (bf16[336,1024]{1,0:T(8,128)(2,1)}, bf16[336,1024]{1,0:T(8,128)(2,1)S(1)}, u32[]{:S(2)}) copy-start(bf16[336,1024]{1,0:T(8,128)(2,1)S(1)} %collective-permute-done.1.high_ref) | copy-start | bytes 2064388

commit v2 on v1

--- a/solution.py
+++ b/solution.py
@@ -70,6 +70,36 @@
     return dot(ah, bh) + dot(ah, bl) + dot(al, bh)
 
 
+def keys_kernel(distance):
+    magnitude = jnp.abs(distance)
+    inner_part = (1.5 * magnitude - 2.5) * magnitude * magnitude + 1.0
+    outer_part = ((-0.5 * magnitude + 2.5) * magnitude - 4.0) * magnitude + 2.0
+    return jnp.where(magnitude <= 1.0, inner_part, jnp.where(magnitude < 2.0, outer_part, 0.0))
+
+
+def field(offset_ref, numbers, across):
+    chip_rows = offset_ref.shape[0] // across
+    centre = (CHIP - 1) * 0.5
+    clipped = jnp.clip(numbers.astype(f32), centre, (chip_rows - 1) * CHIP + centre)
+    result = jnp.zeros(numbers.shape, f32)
+    for k in range(chip_rows):
+        total = offset_ref[k * across]
+        for j in range(1, across):
+            total = total + offset_ref[k * across + j]
+        weight = jnp.maximum(1.0 - jnp.abs(clipped - (k * CHIP + centre)) / CHIP, 0.0)
+        result = result + weight * total.astype(f32)
+    return result / (64.0 * across)
+
+
+def turns(column_ref, valid_ref, numbers, width, across):
+    lane = lax.broadcasted_iota(jnp.int32, numbers.shape, 1)
+    quarter = width // 4
+    frequency = jnp.where(lane < quarter, 2 * lane, 2 * (lane - quarter) + 1).astype(f32)
+    angle = (2.0 * math.pi / width) * frequency * field(column_ref, numbers, across)
+    keep = jnp.where(numbers < valid_ref[0], 1.0, 0.0)
+    return jnp.cos(angle) * keep, jnp.sin(angle) * keep
+
+
 def shift_rows(x, cos, sin, fe, ge, fo, go):
     rows, width = x.shape
     half, quarter = width // 2, width // 4
@@ -93,9 +123,9 @@
 
 def shift_kernel(
     near,
-    resp_ref, x_hbm, tiles_ref, keep_ref, cos_ref, sin_ref, fe, ge, fo, go,
+    resp_ref, column_ref, valid_ref, x_hbm, tiles_ref, fe, ge, fo, go,
     xs_hbm, syn_out, tiles_out,
-    xbuf, obuf, partial, other, total, syn_buf, tile_buf,
+    own_tiles, cos_ref, sin_ref, xbuf, obuf, partial, other, total, syn_buf, tile_buf,
     in_sem, out_sem, pair_sem, syn_send, syn_recv, tile_send, tile_recv,
 ):
     count = lax.axis_size("rows")
@@ -109,6 +139,7 @@
     for copy in in_copies:
         copy.start()
 
+    own_tiles[...] = tiles_ref[...].astype(bf16)
     barrier = pltpu.get_barrier_semaphore()
     for d in range(1, count):
         pl.semaphore_signal(
@@ -120,13 +151,16 @@
     tile_copies = []
     for d in range(1, count):
         copy = pltpu.make_async_remote_copy(
-            src_ref=tiles_ref, dst_ref=tile_buf.at[d], send_sem=tile_send.at[d],
+            src_ref=own_tiles, dst_ref=tile_buf.at[d], send_sem=tile_send.at[d],
             recv_sem=tile_recv.at[d], device_id={"rows": lax.rem(me + d, count)},
             device_id_type=MESH,
         )
         copy.start()
         tile_copies.append(copy)
 
+    across = 2 * width // CHIP - 1
+    numbers = me * height + lax.broadcasted_iota(jnp.int32, cos_ref.shape, 0)
+    cos_ref[...], sin_ref[...] = turns(column_ref, valid_ref, numbers, width, across)
     acc = jnp.zeros((height, width), f32)
     for g in range(steps):
         in_copies[g].wait()
@@ -135,7 +169,8 @@
             return acc + resp_ref[g * group + b] * xbuf[g, b].astype(f32)
 
         acc = lax.fori_loop(0, group, add, acc)
-    partial[...] = (acc * keep_ref[...]).astype(bf16)
+    numbers = me * height + lax.broadcasted_iota(jnp.int32, acc.shape, 0)
+    partial[...] = jnp.where(numbers < valid_ref[0], acc, 0.0).astype(bf16)
     pair = pltpu.make_async_remote_copy(
         src_ref=partial, dst_ref=other, send_sem=pair_sem.at[0], recv_sem=pair_sem.at[1],
         device_id={"bands": 1 - core}, device_id_type=MESH,
@@ -176,7 +211,7 @@
     for d, copy in enumerate(syn_copies, 1):
         copy.wait()
         syn_out[pl.ds(lax.rem(spot + near - d, near), 1)] = syn_buf[d][None]
-    tiles_out[pl.ds(me, 1)] = tiles_ref[...][None]
+    tiles_out[pl.ds(me, 1)] = own_tiles[...][None]
     for d, copy in enumerate(tile_copies, 1):
         copy.wait()
         tiles_out[pl.ds(lax.rem(me + count - d, count), 1)] = tile_buf[d][None]
@@ -185,18 +220,19 @@
 
 
 def corr_kernel(
-    index_ref, syn_ref, tiles_ref, colh, coll, rowh, rowl, backh, backl, lasth, lastl,
+    near, held, owner_ref, slot_ref, device_ref, syn_ref, tiles_ref, colh, coll, rowh, rowl, backh, backl, lasth, lastl,
     out_ref, a_ref,
 ):
     syn = syn_ref[...]
     width = syn.shape[1]
     across = 2 * width // CHIP - 1
     rolled = pltpu.roll(syn.astype(f32), width - CHIP // 2, 1).astype(bf16)
+    first = device_ref[0] // near * across
     chips, tiles = [], []
     for j in range(across):
         source = rolled if j % 2 else syn
         chips.append(source[:, j // 2 * CHIP : (j // 2 + 1) * CHIP])
-        tiles.append(tiles_ref[index_ref[j]])
+        tiles.append(tiles_ref[owner_ref[first + j] * held + slot_ref[first + j]])
 
     def spectra(blocks):
         stacked = jnp.concatenate(blocks, axis=0)
@@ -212,7 +248,7 @@
     xr, xi, yr, yi = x[:CHIP], x[CHIP:], y[:CHIP], y[CHIP:]
     a_ref[:CHIP] = xr * yr + xi * yi
     a_ref[CHIP:] = xi * yr - xr * yi
-    spot = index_ref[across]
+    spot = lax.rem(device_ref[0], near)
     back = dot3((backh[spot], backl[spot]), split(a_ref[...]))
     height = back.shape[0] // 2
     rows = jnp.concatenate(
@@ -234,50 +270,63 @@
 
 
 def resample_kernel(
-    xs_ref, low_ref, high_ref, cos_ref, sin_ref, fe, ge, fo, go, inner_ref, rim_ref,
-    out_ref, halo,
+    height, row_ref, column_ref, valid_ref, device_ref, xs_ref, low_ref, high_ref,
+    fe, ge, fo, go, out_ref, halo, inner_ref, rim_ref,
 ):
     width = xs_ref.shape[1]
     half = width // 2
+    across = 2 * width // CHIP - 1
+    size = PACK * height
 
     @pl.when(pl.program_id(0) == 0)
     def _():
+        first_row = device_ref[0] * height
         steps = halo.shape[0]
+        bands = steps * GROUP
         for side, ref in enumerate((low_ref, high_ref)):
-            left, right = shift_rows(ref[...], cos_ref[side], sin_ref[side], fe, ge, fo, go)
-            size = ref.shape[0] // steps
-            for g in range(steps):
-                rows = slice(g * size, (g + 1) * size)
-                halo[g, side * size : (side + 1) * size, :half] = left[rows]
-                halo[g, side * size : (side + 1) * size, half:] = right[rows]
+            start = first_row + (height if side else -RIM)
+            numbers = start + lax.broadcasted_iota(jnp.int32, (8, half), 0)
+            cos, sin = turns(column_ref, valid_ref, numbers, width, across)
+            for j in range(RIM):
+                left, right = shift_rows(
+                    ref[j * bands : (j + 1) * bands], cos[j : j + 1], sin[j : j + 1],
+                    fe, ge, fo, go,
+                )
+                place = (side * RIM + j) * GROUP
+                for g in range(steps):
+                    rows = slice(g * GROUP, (g + 1) * GROUP)
+                    halo[g, place : place + GROUP, :half] = left[rows]
+                    halo[g, place : place + GROUP, half:] = right[rows]
+
+        def matrix(columns, target, joined):
+            spread = lax.broadcasted_iota(jnp.int32, (size, columns), 0)
+            row = spread & (height - 1)
+            band = spread // height
+            column = lax.broadcasted_iota(jnp.int32, (size, columns), 1)
+            numbers = first_row + row
+            source = row.astype(f32) - field(row_ref, numbers, across)
+            value = keys_kernel(target(column).astype(f32) - source)
+            used = joined(column, band) & (numbers < valid_ref[0])
+            return jnp.where(used, value, 0.0).astype(bf16)
+
+        inner_ref[...] = matrix(
+            size, lambda c: c & (height - 1), lambda c, band: c // height == band
+        )
+
+        def rim_target(c):
+            line = c // GROUP
+            return jnp.where(line < RIM, line - RIM, line - RIM + height)
+
+        for s in range(GROUP // PACK):
+            rim_ref[s] = matrix(
+                2 * RIM * GROUP, rim_target,
+                lambda c, band, s=s: (c & (GROUP - 1)) == band + s * PACK,
+            )
 
     rim = halo[pl.program_id(0)]
-    size = inner_ref.shape[0]
     for s in range(GROUP // PACK):
         rows = slice(s * size, (s + 1) * size)
         out_ref[rows] = (dot(inner_ref[...], xs_ref[rows]) + dot(rim_ref[s], rim)).astype(bf16)
-
-
-def keys_kernel(distance):
-    magnitude = jnp.abs(distance)
-    inner_part = (1.5 * magnitude - 2.5) * magnitude * magnitude + 1.0
-    outer_part = ((-0.5 * magnitude + 2.5) * magnitude - 4.0) * magnitude + 2.0
-    return jnp.where(magnitude <= 1.0, inner_part, jnp.where(magnitude < 2.0, outer_part, 0.0))
-
-
-def offset_fields(row_offset, column_offset, across, first_row, row_count):
-    chip_rows = row_offset.shape[0] // across
-    scale = 64.0 * across
-    row_means = jnp.sum(row_offset.astype(f32).reshape(chip_rows, across), axis=1) / scale
-    column_means = jnp.sum(column_offset.astype(f32).reshape(chip_rows, across), axis=1) / scale
-    centres = jnp.arange(chip_rows, dtype=f32) * CHIP + (CHIP - 1) * 0.5
-    positions = first_row + jnp.arange(row_count, dtype=f32)
-    clipped = jnp.clip(positions, (CHIP - 1) * 0.5, (chip_rows - 1) * CHIP + (CHIP - 1) * 0.5)
-    weights = jnp.maximum(1.0 - jnp.abs(clipped[:, None] - centres[None, :]) / CHIP, 0.0)
-    return (
-        jnp.sum(weights * row_means[None], axis=1),
-        jnp.sum(weights * column_means[None], axis=1),
-    )
 
 
 def on_device(
@@ -296,31 +345,13 @@
 
     forward = [(i, i + 1) for i in range(count - 1)]
     backward = [(i + 1, i) for i in range(count - 1)]
-    low = lax.ppermute(radiance[:, height - RIM :].reshape(bands * RIM, width), "rows", forward)
-    high = lax.ppermute(radiance[:, :RIM].reshape(bands * RIM, width), "rows", backward)
+    low = lax.ppermute(radiance[:, height - RIM :].transpose(1, 0, 2).reshape(bands * RIM, width), "rows", forward)
+    high = lax.ppermute(radiance[:, :RIM].transpose(1, 0, 2).reshape(bands * RIM, width), "rows", backward)
 
     tables = shift_tables(width)
     columns, rows, chip_c, chip_s, last = chip_tables()
 
-    outer = height + 2 * RIM
-    row_shift, column_shift = offset_fields(
-        row_offset, column_offset, across, (first_row - RIM).astype(f32), outer
-    )
-    numbers = first_row - RIM + jnp.arange(outer, dtype=jnp.int32)
-    keep = (numbers < valid_rows[0]).astype(f32)
-    frequency = np.concatenate([np.arange(0, half, 2), np.arange(1, half, 2)]).astype(np.float32)
-    angles = (2.0 * math.pi / width) * frequency[None, :] * column_shift[:, None]
-    turn_cos = jnp.cos(angles) * keep[:, None]
-    turn_sin = jnp.sin(angles) * keep[:, None]
-    own = slice(RIM, RIM + height)
-
-    def rim_turn(turn):
-        sides = jnp.stack([turn[:RIM], turn[RIM + height :]])
-        return jnp.tile(sides, (1, GROUP, 1))
-
-    keep_own = keep[own]
-    shift_own = row_shift[own]
-
+    where = jnp.full((1,), device, jnp.int32)
     vmem = pl.BlockSpec(memory_space=pltpu.VMEM)
     smem = pl.BlockSpec(memory_space=pltpu.SMEM)
     anywhere = pl.BlockSpec(memory_space=pl.ANY)
@@ -333,9 +364,12 @@
             jax.ShapeDtypeStruct((near, height, width), bf16),
             jax.ShapeDtypeStruct((count, tile_count, CHIP, CHIP), bf16),
         ),
-        in_specs=[smem, anywhere] + [vmem] * 8,
+        in_specs=[smem] * 3 + [anywhere] + [vmem] * 5,
         out_specs=(anywhere, vmem, vmem),
         scratch_shapes=[
+            pltpu.VMEM((tile_count, CHIP, CHIP), bf16),
+            pltpu.VMEM((height, half), f32),
+            pltpu.VMEM((height, half), f32),
             pltpu.VMEM((steps, GROUP, height, width), bf16),
             pltpu.VMEM((steps, GROUP * height, width), bf16),
             pltpu.VMEM((height, width), bf16),
@@ -352,17 +386,9 @@
         ),
         name="shift",
     )(
-        response.astype(f32), radiance, reference_tiles.astype(bf16),
-        jnp.broadcast_to(keep_own[:, None], (height, width)),
-        turn_cos[own], turn_sin[own], *tables,
-    )
-
-    chip_row = device // near
-    owner_of = lax.dynamic_slice_in_dim(chip_owner[:, 0], chip_row * across, across)
-    slot_of = lax.dynamic_slice_in_dim(tile_slot, chip_row * across, across)
-    index = jnp.concatenate(
-        [owner_of * tile_count + slot_of, jnp.full((1,), device % near, jnp.int32)]
-    )
+        response.astype(f32), column_offset, valid_rows, radiance, reference_tiles, *tables,
+    )
+
     back = np.stack(
         [
             np.block([[chip_c[u], -chip_s[u]], [chip_s[u], chip_c[u]]])
@@ -370,9 +396,9 @@
         ]
     )
     surface = pl.pallas_call(
-        corr_kernel,
+        functools.partial(corr_kernel, near, tile_count),
         out_shape=jax.ShapeDtypeStruct((height, across * CHIP), f32),
-        in_specs=[smem] + [vmem] * 10,
+        in_specs=[smem] * 3 + [vmem] * 10,
         out_specs=vmem,
         scratch_shapes=[pltpu.VMEM((2 * CHIP, across * CHIP), f32)],
         cost_estimate=pl.CostEstimate(
@@ -380,45 +406,29 @@
         ),
         name="correlate",
     )(
-        index, syn_all.reshape(near * height, width),
+        chip_owner[:, 0], tile_slot, where, syn_all.reshape(near * height, width),
         tiles_all.reshape(count * tile_count, CHIP, CHIP),
         *split_np(columns), *split_np(rows), *split_np(back), *split_np(last),
     )
 
-    size = PACK * height
-    row_of = np.arange(size) % height
-    band_of = np.arange(size) // height
-    source = np.arange(height, dtype=np.float32)
-    place = jnp.tile(source - shift_own, PACK)[:, None]
-    keep_rows = jnp.tile(keep_own, PACK)[:, None]
-    same = (band_of[:, None] == band_of[None, :]).astype(np.float32)
-    inner = (keys_kernel(row_of[None, :].astype(np.float32) - place) * (same * keep_rows)).astype(bf16)
-    rim_band = np.tile(np.repeat(np.arange(GROUP), RIM), 2)
-    rim_row = np.concatenate(
-        [np.tile(np.arange(RIM) - RIM, GROUP), np.tile(np.arange(RIM) + height, GROUP)]
-    ).astype(np.float32)
-    joined = np.stack(
-        [
-            (band_of[:, None] + s * PACK == rim_band[None, :]).astype(np.float32)
-            for s in range(GROUP // PACK)
-        ]
-    )
-    rim = ((keys_kernel(rim_row[None, :] - place) * keep_rows)[None] * joined).astype(bf16)
-
     block = pl.BlockSpec((GROUP * height, width), lambda g: (g, 0))
     aligned = pl.pallas_call(
-        resample_kernel,
+        functools.partial(resample_kernel, height),
         grid=(steps,),
         out_shape=jax.ShapeDtypeStruct((bands * height, width), bf16),
-        in_specs=[block] + [vmem] * 10,
+        in_specs=[smem] * 4 + [block] + [vmem] * 6,
         out_specs=block,
-        scratch_shapes=[pltpu.VMEM((steps, 2 * RIM * GROUP, width), bf16)],
+        scratch_shapes=[
+            pltpu.VMEM((steps, 2 * RIM * GROUP, width), bf16),
+            pltpu.VMEM((PACK * height, PACK * height), bf16),
+            pltpu.VMEM((GROUP // PACK, PACK * height, 2 * RIM * GROUP), bf16),
+        ],
         compiler_params=pltpu.CompilerParams(dimension_semantics=("arbitrary",)),
         cost_estimate=pl.CostEstimate(
             flops=3_000_000_000, bytes_accessed=4 * bands * height * width, transcendentals=0
         ),
         name="resample",
-    )(xs, low, high, rim_turn(turn_cos), rim_turn(turn_sin), *tables, inner, rim)
+    )(row_offset, column_offset, valid_rows, where, xs, low, high, *tables)
     return (aligned.reshape(bands, height, width), surface)
 
 

time: 71.3 us -> 75.9 us (1.065)
  Pallas kernels: 45.9 us -> 61.6 us
  other arithmetic: 7.27 us -> 1.17 us
  local copies, waits for them, and re-layouts: 9.4 us -> 4.59 us
    pallas_call x1, Pallas kernels: 26 us -> 35.8 us  [on_device(): pl.pallas_call(functools.partial(shift_kernel, near), out_shape=(jax.Shap...]
    pallas_call x2, Pallas kernels: 19.8 us -> 25.9 us  [the longest x1 18.9 us: on_device(): pl.pallas_call(functools.partial(resample_kernel, height), grid=(steps,),...]
    convert_element_type x6 -> x0, other arithmetic: 4.43 us -> none  [the longest x1 1.54 us: on_device(): reference_tiles.astype(bf16)]
    slice x4 -> x0, local copies, waits for them, and re-layouts: 4.3 us -> none  [the longest x1 2.95 us: on_device(): radiance[:, :RIM].reshape(bands * RIM, width)]
    transpose x0 -> x3, local copies, waits for them, and re-layouts: none -> 3.45 us  [the longest x2 3.18 us: on_device(): radiance[:, :RIM].transpose(1, 0, 2).reshape(bands * RIM, width)]
    another operation x10 -> x0, local copies, waits for them, and re-layouts: 1.6 us -> none  [the longest x4 1.57 us: rim_turn(): return jnp.tile(sides, (1, GROUP, 1))]
    reshape x4 -> x0, local copies, waits for them, and re-layouts: 1.4 us -> none  [the longest x1 0.62 us: on_device(): radiance[:, height - RIM:].reshape(bands * RIM, width)]
    mul x2 -> x0, other arithmetic: 1.19 us -> none  [the longest x1 1.05 us: on_device(): turn_sin = jnp.sin(angles) * keep[:, None]]
  transfers between devices with their start and end apart: 2 -> 2, of which waited for: 0 -> 0; matrix products, arithmetic and copies ran while one was open for 17% -> 2% of each run, Pallas kernels for 47% -> 57%
where the time goes in v2:
time: 75.9 us; the launch traced here: 75 us
  Pallas kernels  61.6 us (81%)
  starting transfers between devices  6.23 us (8%)
  local copies, waits for them, and re-layouts  4.59 us (6%)
  between operations  1.34 us (2%)
  other arithmetic  1.17 us (2%)
    pallas_call x1, Pallas kernels, on_device(): pl.pallas_call(functools.partial(shift_kernel, near), out_shape=(jax.Shap...  35.8 us
    pallas_call x1, Pallas kernels, on_device(): pl.pallas_call(functools.partial(resample_kernel, height), grid=(steps,),...  18.9 us
    pallas_call x1, Pallas kernels, on_device(): pl.pallas_call(functools.partial(corr_kernel, near, tile_count), out_shap...  6.91 us
    ppermute x1, starting transfers between devices, on_device(): lax.ppermute(radiance[:, height - RIM:].transpose(1, 0, 2).reshape(bands...  4.94 us
    transpose x2, local copies, waits for them, and re-layouts, on_device(): radiance[:, :RIM].transpose(1, 0, 2).reshape(bands * RIM, width)  3.18 us
  transfers between devices with their start and end apart: 2, of which 0 were waited for; matrix products, arithmetic and copies ran while one was open for 2% of the time, Pallas kernels for 57%

profile of v2, /device:TPU:0, one launch (start us, length us, event | category | flops | bytes accessed | tf_op | source)
XLA Modules:
  0.0 75.0 jit_solution(11518792761061125786)
XLA Ops:
  0.6 2.9 %slice_bitcast_fusion = (bf16[3,112,1024]{2,0,1:T(4,128)(2,1)S(1)}, bf16[3,112,1024]{2,0,1:T(4,128)(2,1)S(1)}) fusion(bf16[112,32,1024]{2,1,0:T(8,128)(2,1)} %x_hbm.1), kind=kLoop, calls=%fused_computation | loop fusion | bytes 2752512 | tf_op jit(solution)/shard_map/transpose | solution.py:349
  3.5 0.3 copy.22
  3.8 4.9 %collective-permute-start = (bf16[336,1024]{1,0:T(8,128)(2,1)S(1)}, bf16[336,1024]{1,0:T(8,128)(2,1)S(1)}, u32[]{:S(2)}, u32[]{:S(2)}) collective-permute-start(bf16[336,1024]{1,0:T(8,128)(2,1)S(1)} %bitcast.12), channel_id=1, source_target_pairs={{0,2},{2,4},{4,6},{6,8},{8,10},{10,12},{12,14},{1,3},{3,5},{5,7},{... | collective-permute-start | bytes 2064392 | tf_op jit(solution)/shard_map/ppermute | solution.py:348
  8.8 0.3 copy.23
  9.0 1.3 %collective-permute-start.1 = (bf16[336,1024]{1,0:T(8,128)(2,1)S(1)}, bf16[336,1024]{1,0:T(8,128)(2,1)S(1)}, u32[]{:S(2)}, u32[]{:S(2)}) collective-permute-start(bf16[336,1024]{1,0:T(8,128)(2,1)S(1)} %bitcast.13), channel_id=1, source_target_pairs={{2,0},{4,2},{6,4},{8,6},{10,8},{12,10},{14,12},{3,1},{5,3},{7,5},{... | collective-permute-start | bytes 2064392 | tf_op jit(solution)/shard_map/ppermute | solution.py:349
  11.0 1.2 %convert_element_type.3.resp_ref = f32[112]{0:T(128)} convert(bf16[112]{0:T(256)(128)(2,1)} %param.21) | non-fusion elementwise | flops 112 | bytes 672 | tf_op jit(solution)/shard_map/convert_element_type | solution.py:389
  12.2 35.8 %shift.1 = (bf16[3584,1024]{1,0:T(8,128)(2,1)}, bf16[4,32,1024]{2,1,0:T(8,128)(2,1)}, bf16[8,2,128,128]{3,2,1,0:T(8,128)(2,1)}) custom-call(f32[112]{0:T(128)} %convert_element_type.3.resp_ref, s32[30]{0:T(128)} %column_ref.3, s32[1]{0:T(128)S(6)} %copy.24.valid_ref, bf16[112,32,1024]{2,1,0:T(8,128)(2,1)} %x_hbm.1, f32[2,128,128]{2,1,0:T(8,128)} %tiles_ref.1, ...), custom_call_target="tpu_custom_call" | custom-call | flops 7516192768 | bytes 14680064 | tf_op jit(solution)/shard_map/shift/pallas_call | solution.py:360
  47.9 6.9 %correlate.1 = f32[32,1920]{1,0:T(8,128)} custom-call(s32[30]{0:T(128)} %bitcast.14, s32[30]{0:T(128)} %slot_ref.1, s32[1]{0:T(128)} %bitcast.device_ref, bf16[128,1024]{1,0:T(8,128)(2,1)} %bitcast.16, bf16[16,128,128]{2,1,0:T(8,128)(2,1)} %bitcast.15, bf16[128,256]{1,0:T(8,128)(2,1)} %constant.34.clone.colh, bf16[128,256]{1,0:T(8,128)(2,1)} %constant.35.clone.coll, ...), custom_call_target="tpu_custom_call" | custom-call | flops 2500000000 | bytes 4000000 | tf_op jit(solution)/shard_map/correlate/pallas_call | solution.py:398
  54.8 0.0 collective-permute-done.low_ref
  54.8 0.0 copy-start
  54.8 0.0 collective-permute-done.1.high_ref
  54.9 0.0 copy-start.1
  54.9 0.8 %copy-done = bf16[336,1024]{1,0:T(8,128)(2,1)} copy-done((bf16[336,1024]{1,0:T(8,128)(2,1)}, bf16[336,1024]{1,0:T(8,128)(2,1)S(1)}, u32[]{:S(2)}) %copy-start) | copy-done | bytes 688152
  55.7 0.3 copy-done.1
  56.0 18.9 %resample.1 = bf16[3584,1024]{1,0:T(8,128)(2,1)} custom-call(s32[30]{0:T(128)} %row_ref.1, s32[30]{0:T(128)} %column_ref.3, s32[1]{0:T(128)S(6)} %copy.24.valid_ref, s32[1]{0:T(128)} %bitcast.device_ref, bf16[3584,1024]{1,0:T(8,128)(2,1)} %get-tuple-element.5.xs_ref, bf16[336,1024]{1,0:T(8,128)(2,1)} %copy-done, bf16[336,1024]{1,0:T(8,128)(2,1)} %copy-done.1, ...), custom_call_target="tpu_custom_call" | custom-call | flops 3000000000 | bytes 14680064 | tf_op jit(solution)/shard_map/resample/pallas_call | solution.py:415
Async XLA Ops:
  3.8 51.0 %collective-permute-start = (bf16[336,1024]{1,0:T(8,128)(2,1)S(1)}, bf16[336,1024]{1,0:T(8,128)(2,1)S(1)}, u32[]{:S(2)}, u32[]{:S(2)}) collective-permute-start(bf16[336,1024]{1,0:T(8,128)(2,1)S(1)} %bitcast.12), channel_id=1, source_target_pairs={{0,2},{2,4},{4,6},{6,8},{8,10},{10,12},{12,14},{1,3},{3,5},{5,7},{... | collective-permute-start | bytes 2064392 | tf_op jit(solution)/shard_map/ppermute | solution.py:348
  9.0 45.8 %collective-permute-start.1 = (bf16[336,1024]{1,0:T(8,128)(2,1)S(1)}, bf16[336,1024]{1,0:T(8,128)(2,1)S(1)}, u32[]{:S(2)}, u32[]{:S(2)}) collective-permute-start(bf16[336,1024]{1,0:T(8,128)(2,1)S(1)} %bitcast.13), channel_id=1, source_target_pairs={{2,0},{4,2},{6,4},{8,6},{10,8},{12,10},{14,12},{3,1},{5,3},{7,5},{... | collective-permute-start | bytes 2064392 | tf_op jit(solution)/shard_map/ppermute | solution.py:349
  54.8 0.8 %copy-start = (bf16[336,1024]{1,0:T(8,128)(2,1)}, bf16[336,1024]{1,0:T(8,128)(2,1)S(1)}, u32[]{:S(2)}) copy-start(bf16[336,1024]{1,0:T(8,128)(2,1)S(1)} %collective-permute-done.low_ref) | copy-start | bytes 2064388
  54.9 1.2 %copy-start.1 = (bf16[336,1024]{1,0:T(8,128)(2,1)}, bf16[336,1024]{1,0:T(8,128)(2,1)S(1)}, u32[]{:S(2)}) copy-start(bf16[336,1024]{1,0:T(8,128)(2,1)S(1)} %collective-permute-done.1.high_ref) | copy-start | bytes 2064388
